TPU v7x, 256 devices: a whole 4x4x8 slice. The times are simulated.
256 devices in a mesh: blk: 32 (over y, z), row: 8 (over x, core).
Axes of the slice: x: 4, y: 4, z: 8, core: 2. Of those that a mesh axis runs over, the one named last changes fastest.
Arguments:
- far_kernel: bfloat16 [256, 8, 512, 512], P('blk', None, 'row'), may hold values from -0.25 to 0.25
- near_kernel: bfloat16 [256, 2, 512, 512], P('blk', None, 'row'), may hold values from -0.25 to 0.25
- samples: bfloat16 [256, 512, 128], P('blk'), may hold values from -18 to 18
- far_target: int32 [256, 8], P('blk'), may hold values from 0 to 255, as said below
Outputs:
- basis_out: float32 [256, 512, 128], P('blk', 'row')
- coupling: float32 [256, 8, 128, 128], P('blk', None, 'row')
- parent_samples: float32 [128, 256, 128], P('blk', 'row')
Inputs may be any that keep to these rules, and one draw needn't show every extreme that they name: `far_target`: each row names 8 different target clusters; among the far blocks of the source clusters of one index of blk (rows 8 * g to 8 * g + 7), at most 4 name targets of any one index of blk (clusters 8 * h to 8 * h + 7), and exactly 4 for some such index.
All inputs are finite; a program needn't handle non-finite values.
Results may differ from a plain program's by a relative error of at most 0.02.
Values may be sent and summed in bfloat16 or wider, within the bound.
No kernel may reach another device: no remote copies, remote signals or barrier semaphores. Data moves between devices by JAX's collectives and lax.ppermute only.
A program may use at most 64 MiB of HBM per device.

v0:
```python
import jax
import jax.numpy as jnp
from jax import lax
from jax.sharding import PartitionSpec as P

ITERS = 12


def inverse_root(gram_mat, full_width):
    highest = lax.Precision.HIGHEST
    sample_cols = gram_mat.shape[-1]
    identity = jnp.eye(sample_cols, dtype=jnp.float32)
    mean_sq = jnp.trace(gram_mat, axis1=1, axis2=2) / (full_width * sample_cols) + 1e-06
    level_mat = gram_mat / (full_width * sample_cols * mean_sq)[:, None, None]
    root_mat = jnp.broadcast_to(identity, gram_mat.shape)
    for sweep_index in range(ITERS):
        step_mat = 1.5 * identity - 0.5 * jnp.matmul(root_mat, level_mat, precision=highest)
        level_mat = jnp.matmul(level_mat, step_mat, precision=highest)
        root_mat = jnp.matmul(step_mat, root_mat, precision=highest)
    return root_mat / jnp.sqrt(sample_cols * mean_sq)[:, None, None]


def per_device(far_kernel, near_kernel, samples, far_target):
    highest = lax.Precision.HIGHEST
    local_count, far_count, row_count, full_width = far_kernel.shape
    sample_cols = samples.shape[2]
    row_offset = lax.axis_index("row") * row_count
    targets = far_target.reshape(local_count * far_count)
    flat_width = row_count * sample_cols
    products = jnp.einsum("cfrw,cws->cfrs", far_kernel, samples, preferred_element_type=jnp.float32)
    products = products.astype(jnp.bfloat16).reshape(local_count * far_count, flat_width)
    target_ids = lax.iota(jnp.int32, local_count * lax.axis_size("blk"))
    onehot = (target_ids[:, None] == targets[None, :]).astype(jnp.bfloat16)
    far_sketch = lax.psum_scatter(
        jnp.dot(onehot, products, preferred_element_type=jnp.float32).astype(jnp.bfloat16),
        "blk",
        scatter_dimension=0,
        tiled=True,
    ).astype(jnp.float32)
    sibling = samples.reshape(local_count // 2, 2, full_width, sample_cols)[:, ::-1].reshape(
        local_count, full_width, sample_cols
    )
    paired = jnp.stack([samples, sibling], axis=1)
    near_sum = jnp.einsum("ckrw,ckws->crs", near_kernel, paired, preferred_element_type=jnp.float32)
    sketch = far_sketch.reshape(local_count, row_count, sample_cols) - near_sum
    gram_part = jnp.einsum("crs,crt->cst", sketch, sketch, precision=highest)
    gram_mat = lax.psum(gram_part, "row")
    root_mat = inverse_root(gram_mat, full_width)
    basis_out = jnp.einsum("crs,cst->crt", sketch, root_mat, precision=highest)
    basis_half = basis_out.astype(jnp.bfloat16)
    start_sum = jnp.zeros((local_count, far_count, row_count, sample_cols), jnp.float32)
    segment = lax.all_gather(basis_half, "row", axis=1, tiled=True)
    columns = lax.slice_in_dim(far_kernel, 0, segment.shape[1], axis=3)
    mixed_rows = (
        start_sum
        + jnp.einsum("cfrw,cws->cfrs", columns, segment, preferred_element_type=jnp.float32)
    ).astype(jnp.bfloat16)
    basis_every = lax.all_gather(basis_half, "blk", axis=0, tiled=True)
    picked = jnp.take(basis_every, targets, axis=0).reshape(
        local_count, far_count, row_count, sample_cols
    )
    scale_root = jnp.sqrt(jnp.float32(full_width))
    own_samples = lax.dynamic_slice_in_dim(samples, row_offset, row_count, 1)
    parent_part = (
        jnp.einsum("crs,crt->cst", basis_half, own_samples, preferred_element_type=jnp.float32)
        / scale_root
    )
    parent_part = parent_part.reshape(local_count // 2, 2 * sample_cols, sample_cols)
    coupling_part = (
        jnp.einsum("cfrs,cfrt->cfst", picked, mixed_rows, preferred_element_type=jnp.float32)
        / scale_root
    )
    coupling, parent_samples = (
        lax.psum_scatter(coupling_part, "row", scatter_dimension=2, tiled=True),
        lax.psum_scatter(parent_part, "row", scatter_dimension=1, tiled=True),
    )
    return (basis_out, coupling, parent_samples)


def solution(mesh):
    return jax.shard_map(
        per_device,
        mesh=mesh,
        in_specs=(
            P("blk", None, "row", None),
            P("blk", None, "row", None),
            P("blk", None, None),
            P("blk", None),
        ),
        out_specs=(P("blk", "row", None), P("blk", None, "row", None), P("blk", "row", None)),
        check_vma=False,
    )
```

profile of v0, /device:TPU:8, one launch (start us, length us, event | category | flops | bytes accessed | tf_op | source)
XLA Modules:
  0.0 529.5 jit_solution(16602669929706069161)
XLA Ops:
  7.2 0.8 eq.53
  8.1 3.7 fusion.4
  11.8 3.2 convolution_convert_fusion
  15.2 225.7 %reduce-scatter.4.cloned.1.call-done = bf16[8,8192]{1,0:T(8,128)(2,1)} async-done(((bf16[256,8192]{1,0:T(8,128)(2,1)}), bf16[8,8192]{1,0:T(8,128)(2,1)}) %reduce-scatter.4.cloned.1.call-update) | async-done | bytes 131088 | tf_op jit(solution)/shard_map/reduce_scatter | solution.py:34
  240.9 0.9 bitcast_convert_fusion
  242.4 1.8 fusion.45
  244.5 65.0 %all-reduce.2.cloned.1.call-done = f32[8,128,128]{2,1,0:T(8,128)} async-done(((f32[8,128,128]{2,1,0:T(8,128)}), f32[8,128,128]{2,1,0:T(8,128)}) %all-reduce.2.cloned.1.call-update) | async-done | bytes 524304 | tf_op jit(solution)/shard_map/psum | solution.py:47
  309.5 1.2 select_reduce_fusion
  310.7 1.7 fusion.17
  313.0 1.7 fusion.36
  314.7 0.6 fusion.16
  315.4 0.6 fusion.47
  316.0 0.6 fusion.46
  316.7 0.6 fusion.15
  317.3 0.6 fusion.49
  318.0 0.6 fusion.48
  318.6 0.6 fusion.14
  319.3 0.6 fusion.51
  320.0 0.6 fusion.50
  320.6 0.6 fusion.13
  321.3 0.6 fusion.53
  321.9 0.6 fusion.52
  322.6 0.6 fusion.12
  323.2 0.6 fusion.55
  323.9 0.9 fusion.54
  324.8 0.6 fusion.11
  325.4 0.6 fusion.57
  326.7 0.6 fusion.10
  327.4 0.6 fusion.59
  328.0 0.6 fusion.58
  328.7 0.6 fusion.9
  329.4 0.6 fusion.61
  330.0 0.6 fusion.60
  330.7 0.6 fusion.8
  331.3 0.6 fusion.63
  332.0 0.6 fusion.62
  332.6 0.6 fusion.7
  334.0 0.6 fusion.65
  334.6 0.6 fusion.6
  335.3 0.6 convolution_divide_fusion
  335.9 1.6 fusion.44
  338.3 2.0 convolution_multiply_fusion.1
  340.4 77.0 %all-gather.3.cloned.1.call-done = bf16[256,64,128]{2,1,0:T(8,128)(2,1)} async-done(((bf16[8,64,128]{2,1,0:T(8,128)(2,1)}), bf16[256,64,128]{2,1,0:T(8,128)(2,1)}) %all-gather.3.cloned.1.call-update) | async-done | bytes 4194320 | tf_op jit(solution)/shard_map/all_gather | solution.py:58
  417.4 2.9 gather_fusion
  420.4 23.2 %all-gather.5.cloned.1.call-done = bf16[8,512,128]{2,1,0:T(8,128)(2,1)} async-done(((bf16[8,64,128]{2,1,0:T(8,128)(2,1)}), bf16[8,512,128]{2,1,0:T(8,128)(2,1)}) %all-gather.5.cloned.1.call-update) | async-done | bytes 1048592 | tf_op jit(solution)/shard_map/all_gather | solution.py:52
  443.5 6.3 %convolution_multiply_fusion = f32[8,8,128,128]{3,2,1,0:T(8,128)} fusion(bf16[8,8,64,512]{3,2,1,0:T(8,128)(2,1)} %param.4, bf16[8,512,128]{2,1,0:T(8,128)(2,1)} %all-gather.5.cloned.1.call-done, bf16[8,8,64,128]{3,2,1,0:T(8,128)(2,1)S(1)} %bitcast.112, pred[8,8]{1,0:T(8,128)(4,1)S(1)} %compare_and_fusion), kind=kOutput, calls=%fused_computation.2 | convolution fusion | flops 673185792 | bytes 10485824 | tf_op jit(solution)/shard_map/cfrs,cfrt->cfst/dot_general | solution.py:70
  449.8 30.5 %reduce-scatter.8.cloned.1.call-done = f32[4,32,128]{2,1,0:T(8,128)} async-done(((f32[4,256,128]{2,1,0:T(8,128)}), f32[4,32,128]{2,1,0:T(8,128)}) %reduce-scatter.8.cloned.1.call-update) | async-done | bytes 65552 | tf_op jit(solution)/shard_map/reduce_scatter | solution.py:75
  480.3 42.4 %reduce-scatter.6.cloned.1.call-done = f32[8,8,16,128]{3,2,1,0:T(8,128)} async-done(((f32[8,8,128,128]{3,2,1,0:T(8,128)}), f32[8,8,16,128]{3,2,1,0:T(8,128)}) %reduce-scatter.6.cloned.1.call-update) | async-done | bytes 524304 | tf_op jit(solution)/shard_map/reduce_scatter | solution.py:74
  (31 shorter events, 3.7 us)
Async XLA Ops:
  7.2 234.6 %copy-start = (bf16[8,2,64,512]{3,2,1,0:T(8,128)(2,1)S(1)}, bf16[8,2,64,512]{3,2,1,0:T(8,128)(2,1)}, u32[]{:S(2)}) copy-start(bf16[8,2,64,512]{3,2,1,0:T(8,128)(2,1)} %param.5) | copy-start | bytes 3145732
  7.2 233.7 %reduce-scatter.4.cloned.1.call-start = ((), (), s32[]{:S(2)}) async-start(), calls=%async_computation.3 | async-start | bytes 4325376 | tf_op jit(solution)/shard_map/reduce_scatter | solution.py:34
  11.8 3.3 copy-start.1
  15.1 294.4 %all-reduce.2.cloned.1.call-start = ((), (), s32[]{:S(2)}) async-start(), calls=%async_computation.4 | async-start | bytes 1048576 | tf_op jit(solution)/shard_map/psum | solution.py:47
  244.2 173.2 %all-gather.3.cloned.1.call-start = ((), (), s32[]{:S(2)}) async-start(), calls=%async_computation.5 | async-start | bytes 4325376 | tf_op jit(solution)/shard_map/all_gather | solution.py:58
  333.3 4.9 copy-start.2
  337.5 106.0 %all-gather.5.cloned.1.call-start = ((), (), s32[]{:S(2)}) async-start(), calls=%async_computation.6 | async-start | bytes 1179648 | tf_op jit(solution)/shard_map/all_gather | solution.py:52
  338.1 142.2 %reduce-scatter.8.cloned.1.call-start = ((), (), s32[]{:S(2)}) async-start(), calls=%async_computation.8 | async-start | bytes 589824 | tf_op jit(solution)/shard_map/reduce_scatter | solution.py:75
  340.3 182.4 %reduce-scatter.6.cloned.1.call-start = ((), (), s32[]{:S(2)}) async-start(), calls=%async_computation.7 | async-start | bytes 4718592 | tf_op jit(solution)/shard_map/reduce_scatter | solution.py:74
Sparse Core Ops, SparseCore 0:
  15.2 225.6 reduce-scatter.3
  244.3 65.1 all-reduce.1
  337.7 79.6 all-gather.2
  419.7 23.8 all-gather.4
  446.5 33.7 reduce-scatter.7
  483.3 39.3 reduce-scatter.5
where the time goes:
time: 530 us
  waiting for transfers between devices  464 us (88%)
  matrix products  44.1 us (8%)
  between operations  14.5 us (3%)
    reduce_scatter x1, waiting for transfers between devices, per_device(): lax.psum_scatter(jnp.dot(onehot, products, preferred_element_type=jnp.flo...  226 us
    all_gather x1, waiting for transfers between devices, per_device(): basis_every = lax.all_gather(basis_half, 'blk', axis=0, tiled=True)  77 us
    psum x1, waiting for transfers between devices, per_device(): gram_mat = lax.psum(gram_part, 'row')  65 us
    reduce_scatter x1, waiting for transfers between devices, per_device(): lax.psum_scatter(coupling_part, 'row', scatter_dimension=2, tiled=True)  42.4 us
    reduce_scatter x1, waiting for transfers between devices, per_device(): lax.psum_scatter(parent_part, 'row', scatter_dimension=1, tiled=True)  30.5 us
    all_gather x1, waiting for transfers between devices, per_device(): segment = lax.all_gather(basis_half, 'row', axis=1, tiled=True)  23.2 us
  transfers between devices with their start and end apart: 6, of which 6 were waited for; matrix products, arithmetic and copies ran while one was open for 2% of the time, Pallas kernels for 0%

commit v1 on v0

--- a/solution.py
+++ b/solution.py
@@ -44,7 +44,7 @@
     near_sum = jnp.einsum("ckrw,ckws->crs", near_kernel, paired, preferred_element_type=jnp.float32)
     sketch = far_sketch.reshape(local_count, row_count, sample_cols) - near_sum
     gram_part = jnp.einsum("crs,crt->cst", sketch, sketch, precision=highest)
-    gram_mat = lax.psum(gram_part, "row")
+    gram_mat = jnp.sum(lax.all_gather(gram_part, "row"), axis=0)
     root_mat = inverse_root(gram_mat, full_width)
     basis_out = jnp.einsum("crs,cst->crt", sketch, root_mat, precision=highest)
     basis_half = basis_out.astype(jnp.bfloat16)

time: 530 us -> 498 us (0.940)
  waiting for transfers between devices: 464 us -> 434 us
    psum x1 -> x0, waiting for transfers between devices: 65 us -> none  [per_device(): gram_mat = lax.psum(gram_part, 'row')]
    all_gather x0 -> x1, waiting for transfers between devices: none -> 33.5 us  [per_device(): gram_mat = jnp.sum(lax.all_gather(gram_part, 'row'), axis=0)]
where the time goes in v1:
time: 498 us
  waiting for transfers between devices  434 us (87%)
  matrix products  42 us (8%)
  between operations  14.5 us (3%)
    reduce_scatter x1, waiting for transfers between devices, per_device(): lax.psum_scatter(jnp.dot(onehot, products, preferred_element_type=jnp.flo...  226 us
    all_gather x1, waiting for transfers between devices, per_device(): basis_every = lax.all_gather(basis_half, 'blk', axis=0, tiled=True)  77.8 us
    reduce_scatter x1, waiting for transfers between devices, per_device(): lax.psum_scatter(coupling_part, 'row', scatter_dimension=2, tiled=True)  42.4 us
    all_gather x1, waiting for transfers between devices, per_device(): gram_mat = jnp.sum(lax.all_gather(gram_part, 'row'), axis=0)  33.5 us
    reduce_scatter x1, waiting for transfers between devices, per_device(): lax.psum_scatter(parent_part, 'row', scatter_dimension=1, tiled=True)  30.5 us
    all_gather x1, waiting for transfers between devices, per_device(): segment = lax.all_gather(basis_half, 'row', axis=1, tiled=True)  23.2 us
  transfers between devices with their start and end apart: 6, of which 6 were waited for; matrix products, arithmetic and copies ran while one was open for 2% of the time, Pallas kernels for 0%

profile of v1, /device:TPU:8, one launch (start us, length us, event | category | flops | bytes accessed | tf_op | source)
XLA Modules:
  0.0 498.2 jit_solution(11571268331857569269)
XLA Ops:
  7.2 0.8 eq.53
  8.1 3.7 fusion.4
  11.8 3.2 convolution_convert_fusion
  15.2 225.7 %reduce-scatter.4.cloned.1.call-done = bf16[8,8192]{1,0:T(8,128)(2,1)} async-done(((bf16[256,8192]{1,0:T(8,128)(2,1)}), bf16[8,8192]{1,0:T(8,128)(2,1)}) %reduce-scatter.4.cloned.1.call-update) | async-done | bytes 131088 | tf_op jit(solution)/shard_map/reduce_scatter | solution.py:34
  240.9 0.9 bitcast_convert_fusion
  242.4 1.8 fusion.45
  244.5 33.5 %all-gather.9.cloned.1.call-done = f32[64,128,128]{2,1,0:T(8,128)} async-done(((f32[8,128,128]{2,1,0:T(8,128)}), f32[64,128,128]{2,1,0:T(8,128)}) %all-gather.9.cloned.1.call-update) | async-done | bytes 4194320 | tf_op jit(solution)/shard_map/all_gather | solution.py:47
  277.9 2.5 reduce_sum.19
  280.6 0.7 fusion.17
  281.3 0.7 fusion.36
  282.6 0.6 fusion.16
  283.2 0.6 fusion.47
  283.9 0.6 fusion.46
  284.5 0.6 fusion.15
  285.2 0.6 fusion.49
  285.8 0.6 fusion.48
  286.5 0.6 fusion.14
  287.2 0.6 fusion.51
  287.8 0.6 fusion.50
  288.5 0.6 fusion.13
  289.1 0.6 fusion.53
  289.8 0.6 fusion.52
  290.4 0.6 fusion.12
  291.1 0.6 fusion.55
  291.7 0.9 fusion.54
  292.6 0.6 fusion.11
  293.9 0.6 fusion.56
  294.6 0.6 fusion.10
  295.2 0.6 fusion.59
  296.5 0.6 fusion.9
  297.2 0.6 fusion.61
  297.9 0.6 fusion.60
  298.5 0.6 fusion.8
  299.2 0.6 fusion.63
  299.8 0.6 fusion.62
  300.5 0.6 fusion.7
  301.1 0.6 fusion.64
  301.8 0.6 fusion.65
  302.5 0.6 fusion.6
  303.1 0.6 convolution_divide_fusion
  303.8 1.6 fusion.44
  306.1 2.0 convolution_multiply_fusion.1
  308.2 77.8 %all-gather.5.cloned.1.call-done = bf16[256,64,128]{2,1,0:T(8,128)(2,1)} async-done(((bf16[8,64,128]{2,1,0:T(8,128)(2,1)}), bf16[256,64,128]{2,1,0:T(8,128)(2,1)}) %all-gather.5.cloned.1.call-update) | async-done | bytes 4194320 | tf_op jit(solution)/shard_map/all_gather | solution.py:58
  386.0 2.9 gather_fusion
  389.0 23.2 %all-gather.7.cloned.1.call-done = bf16[8,512,128]{2,1,0:T(8,128)(2,1)} async-done(((bf16[8,64,128]{2,1,0:T(8,128)(2,1)}), bf16[8,512,128]{2,1,0:T(8,128)(2,1)}) %all-gather.7.cloned.1.call-update) | async-done | bytes 1048592 | tf_op jit(solution)/shard_map/all_gather | solution.py:52
  412.2 6.3 %convolution_multiply_fusion = f32[8,8,128,128]{3,2,1,0:T(8,128)} fusion(bf16[8,8,64,512]{3,2,1,0:T(8,128)(2,1)} %param.4, bf16[8,512,128]{2,1,0:T(8,128)(2,1)} %all-gather.7.cloned.1.call-done, bf16[8,8,64,128]{3,2,1,0:T(8,128)(2,1)S(1)} %bitcast.114, pred[8,8]{1,0:T(8,128)(4,1)S(1)} %compare_and_fusion), kind=kOutput, calls=%fused_computation.2 | convolution fusion | flops 673185792 | bytes 10485824 | tf_op jit(solution)/shard_map/cfrs,cfrt->cfst/dot_general | solution.py:70
  418.4 30.5 %reduce-scatter.8.cloned.1.call-done = f32[4,32,128]{2,1,0:T(8,128)} async-done(((f32[4,256,128]{2,1,0:T(8,128)}), f32[4,32,128]{2,1,0:T(8,128)}) %reduce-scatter.8.cloned.1.call-update) | async-done | bytes 65552 | tf_op jit(solution)/shard_map/reduce_scatter | solution.py:75
  448.9 42.4 %reduce-scatter.6.cloned.1.call-done = f32[8,8,16,128]{3,2,1,0:T(8,128)} async-done(((f32[8,8,128,128]{3,2,1,0:T(8,128)}), f32[8,8,16,128]{3,2,1,0:T(8,128)}) %reduce-scatter.6.cloned.1.call-update) | async-done | bytes 524304 | tf_op jit(solution)/shard_map/reduce_scatter | solution.py:74
  (32 shorter events, 3.8 us)
Async XLA Ops:
  7.2 234.6 %copy-start = (bf16[8,2,64,512]{3,2,1,0:T(8,128)(2,1)S(1)}, bf16[8,2,64,512]{3,2,1,0:T(8,128)(2,1)}, u32[]{:S(2)}) copy-start(bf16[8,2,64,512]{3,2,1,0:T(8,128)(2,1)} %param.5) | copy-start | bytes 3145732
  7.2 233.7 %reduce-scatter.4.cloned.1.call-start = ((), (), s32[]{:S(2)}) async-start(), calls=%async_computation.3 | async-start | bytes 4325376 | tf_op jit(solution)/shard_map/reduce_scatter | solution.py:34
  11.8 3.3 copy-start.1
  15.1 262.9 %all-gather.9.cloned.1.call-start = ((), (), s32[]{:S(2)}) async-start(), calls=%async_computation.8 | async-start | bytes 4718592 | tf_op jit(solution)/shard_map/all_gather | solution.py:47
  244.2 141.9 %all-gather.5.cloned.1.call-start = ((), (), s32[]{:S(2)}) async-start(), calls=%async_computation.4 | async-start | bytes 4325376 | tf_op jit(solution)/shard_map/all_gather | solution.py:58
  301.1 4.9 copy-start.2
  305.4 106.8 %all-gather.7.cloned.1.call-start = ((), (), s32[]{:S(2)}) async-start(), calls=%async_computation.5 | async-start | bytes 1179648 | tf_op jit(solution)/shard_map/all_gather | solution.py:52
  306.0 143.0 %reduce-scatter.8.cloned.1.call-start = ((), (), s32[]{:S(2)}) async-start(), calls=%async_computation.7 | async-start | bytes 589824 | tf_op jit(solution)/shard_map/reduce_scatter | solution.py:75
  308.1 183.2 %reduce-scatter.6.cloned.1.call-start = ((), (), s32[]{:S(2)}) async-start(), calls=%async_computation.6 | async-start | bytes 4718592 | tf_op jit(solution)/shard_map/reduce_scatter | solution.py:74
Sparse Core Ops, SparseCore 0:
  15.2 225.6 reduce-scatter.3
  244.3 33.6 all-gather.8
  305.5 80.4 all-gather.4
  388.3 23.8 all-gather.6
  415.1 33.7 reduce-scatter.7
  451.9 39.3 reduce-scatter.5
